TPU v7x, 32 devices: a whole 2x2x4 slice. The times are simulated.
32 devices in a mesh: fsdp: 4 (over x, core), ctx: 2 (over y), tp: 4 (over z).
Axes of the slice: x: 2, y: 2, z: 4, core: 2. Of those that a mesh axis runs over, the one named last changes fastest.
Arguments:
- inputs: bfloat16 [2048, 8, 768], P('ctx', 'fsdp'), may hold values from -6 to 6
- thoughts: bfloat16 [6, 8, 768], P(None, 'fsdp'), may hold values from -6 to 6
- positions: int32 [6, 8], P(None, 'fsdp'), may hold values from 0 to 2047, as said below
- lengths: int32 [8, 3], P('fsdp'), may hold values from 1 to 1024, 2048 in all within a row
- w_qkv: bfloat16 [3, 768, 768], P(None, 'fsdp', 'tp'), may hold values from -0.21875 to 0.21875
- w_out: bfloat16 [768, 768], P('tp', 'fsdp'), may hold values from -3.5 to 3.5
- w_fc: bfloat16 [768, 3072], P('fsdp', 'tp'), may hold values from -0.21875 to 0.21875
- w_proj: bfloat16 [3072, 768], P('tp', 'fsdp'), may hold values from -0.109375 to 0.109375
- norm_gains: bfloat16 [2, 768], P(None, 'fsdp'), may hold values from 0.099609375 to 1.8984375
- norm_biases: bfloat16 [2, 768], P(None, 'fsdp'), may hold values from -0.14941406 to 0.14941406
- out_grad: bfloat16 [2048, 8, 768], P('ctx', 'fsdp'), may hold values from -6 to 6
Outputs:
- output: bfloat16 [2048, 8, 768], P('ctx', 'fsdp')
- d_inputs: float32 [2048, 8, 768], P('ctx', 'fsdp')
- d_thoughts: float32 [6, 8, 768], P(None, 'fsdp')
- d_w_qkv: float32 [3, 768, 768], P(None, 'fsdp', 'tp')
- d_w_out: float32 [768, 768], P('tp', 'fsdp')
- d_w_fc: float32 [768, 3072], P('fsdp', 'tp')
- d_w_proj: float32 [3072, 768], P('tp', 'fsdp')
- d_norm_gains: float32 [2, 768], P(None, 'fsdp')
- d_bias_first: float32 [768], P('fsdp')
- d_bias_second: float32 [768], P('fsdp')
Inputs may be any that keep to these rules, and one draw needn't show every extreme that they name: Each entry is a position of its sequence; the 6 positions of one sequence are distinct.
All inputs are finite; a program needn't handle non-finite values.
Results may differ from a plain program's by a relative error of at most 0.017.
Values may be sent and summed in bfloat16 or wider, within the bound.
A program may use at most 192 MiB of HBM per device.

v0:
```python
import jax
import jax.numpy as jnp
from jax import lax
from jax.sharding import PartitionSpec as P

HEAD_DIM = 64
EPSILON = 1e-05
NEGATIVE = -1000000000.0
PRECISE = lax.Precision.HIGHEST


def norm_rows(values, gain_row, offset):
    centre = jnp.mean(values, axis=-1, keepdims=True)
    shifted = values - centre
    spread = jnp.mean(shifted * shifted, axis=-1, keepdims=True)
    return shifted * lax.rsqrt(spread + EPSILON) * gain_row + offset


def gelu_tanh(values):
    return jax.nn.gelu(values, approximate=True)


def segment_ids(lengths, length):
    doc_ends = jnp.cumsum(lengths, axis=1, dtype=jnp.int32)
    places = jnp.arange(length, dtype=jnp.int32)
    return jnp.sum((places[:, None, None] >= doc_ends[None, :, :]).astype(jnp.int32), axis=2)


def seq_group(source, block_index, group_size):
    return lax.dynamic_slice_in_dim(source, block_index * group_size, group_size, 1)


def ungroup(stacked, row_count, seq_count):
    return jnp.moveaxis(stacked, 0, 1).reshape(row_count, seq_count, -1)


def heads_first(values):
    return jnp.moveaxis(values, 2, 0)


def heads_back(values):
    return jnp.moveaxis(values, 0, 2)


def score_head(query_head, key_head, query_pos, key_pos, query_seg, key_seg, score_scale):
    scores = (
        jnp.einsum("qgd,kgd->gqk", query_head, key_head, preferred_element_type=jnp.float32)
        * score_scale
    )
    causal = query_pos[:, None] >= key_pos[None, :]
    same_doc = query_seg.T[:, :, None] == key_seg.T[:, None, :]
    allowed = causal[None] & same_doc
    return (jnp.where(allowed, scores, NEGATIVE), allowed)


def head_back(
    query_head,
    key_head,
    value_head,
    grad_head,
    log_head,
    query_pos,
    key_pos,
    query_seg,
    key_seg,
    score_scale,
):
    scores, allowed = score_head(
        query_head, key_head, query_pos, key_pos, query_seg, key_seg, score_scale
    )
    attn_probs = jnp.where(allowed, jnp.exp(scores - log_head[..., None]), 0.0)
    d_probs = jnp.einsum("qgd,kgd->gqk", grad_head, value_head, preferred_element_type=jnp.float32)
    row_delta = jnp.sum(attn_probs * d_probs, axis=-1)
    d_scores = (attn_probs * (d_probs - row_delta[..., None])).astype(jnp.bfloat16)
    d_query = (
        jnp.einsum("gqk,kgd->qgd", d_scores, key_head, preferred_element_type=jnp.float32)
        * score_scale
    )
    d_keys = (
        jnp.einsum("gqk,qgd->kgd", d_scores, query_head, preferred_element_type=jnp.float32)
        * score_scale
    )
    d_values = jnp.einsum(
        "gqk,qgd->kgd",
        attn_probs.astype(jnp.bfloat16),
        grad_head,
        preferred_element_type=jnp.float32,
    )
    return (d_query, row_delta, d_keys, d_values)


def local(
    inputs,
    thoughts,
    positions,
    lengths,
    w_qkv,
    w_out,
    w_fc,
    w_proj,
    norm_gains,
    norm_biases,
    out_grad,
):
    row_count, seq_count, model_width = inputs.shape
    ctx_count = lax.axis_size("ctx")
    seq_length = row_count * ctx_count
    first_row = lax.axis_index("ctx") * row_count
    group_size = max(1, min(seq_count, 512 // row_count))
    block_count = seq_count // group_size
    token_count = row_count * seq_count
    score_scale = HEAD_DIM ** (-0.5)
    qkv_full, out_full, fc_full, proj_full, gain_rows, offset_rows = (
        lax.all_gather(w_qkv, "fsdp", axis=1, tiled=True),
        lax.all_gather(w_out, "fsdp", axis=1, tiled=True),
        lax.all_gather(w_fc, "fsdp", axis=0, tiled=True),
        lax.all_gather(w_proj, "fsdp", axis=1, tiled=True),
        lax.all_gather(norm_gains, "fsdp", axis=1, tiled=True),
        lax.all_gather(norm_biases, "fsdp", axis=1, tiled=True),
    )
    gain_rows = gain_rows.astype(jnp.float32)
    offset_rows = offset_rows.astype(jnp.float32)
    local_width = qkv_full.shape[2]
    local_heads = local_width // HEAD_DIM
    qkv_matrix = jnp.transpose(qkv_full, (1, 0, 2)).reshape(model_width, 3 * local_width)
    row_places = first_row + jnp.arange(row_count, dtype=jnp.int32)
    key_places = jnp.arange(seq_length, dtype=jnp.int32)
    select = (row_places[:, None, None] == positions[None, :, :]).astype(jnp.float32)
    keep_rows = 1.0 - jnp.sum(select, axis=1)
    start_rows = inputs.astype(jnp.float32) * keep_rows[:, :, None] + jnp.einsum(
        "rts,tsd->rsd", select, thoughts.astype(jnp.float32), precision=PRECISE
    )
    start_flat = start_rows.reshape(token_count, model_width)
    normed = norm_rows(start_flat, gain_rows[0], offset_rows[0]).astype(jnp.bfloat16)
    projected = jnp.dot(normed, qkv_matrix, preferred_element_type=jnp.float32)
    queries = (
        projected[:, :local_width]
        .astype(jnp.bfloat16)
        .reshape(row_count, seq_count, local_heads, HEAD_DIM)
    )
    keys_values = (
        projected[:, local_width:]
        .astype(jnp.bfloat16)
        .reshape(row_count, seq_count, 2 * local_width)
    )
    seg_all = segment_ids(lengths, seq_length)
    seg_rows = lax.dynamic_slice_in_dim(seg_all, first_row, row_count, 0)

    def split_pairs(whole_kv, count):
        key_part = whole_kv[..., :local_width].reshape(count, group_size, local_heads, HEAD_DIM)
        value_part = whole_kv[..., local_width:].reshape(count, group_size, local_heads, HEAD_DIM)
        return (key_part, value_part)

    def forward_block(block_index):
        whole_kv = lax.all_gather(
            seq_group(keys_values, block_index, group_size), "ctx", axis=0, tiled=True
        )
        key_part, value_part = split_pairs(whole_kv, seq_length)
        query_seg = seq_group(seg_rows, block_index, group_size)
        key_seg = seq_group(seg_all, block_index, group_size)

        def forward_one_head(triple):
            query_head, key_head, value_head = triple
            scores, allowed = score_head(
                query_head, key_head, row_places, key_places, query_seg, key_seg, score_scale
            )
            top_score = jnp.max(scores, axis=-1, keepdims=True)
            raised = jnp.exp(scores - top_score)
            row_total = jnp.sum(raised, axis=-1, keepdims=True)
            attn_probs = (raised / row_total).astype(jnp.bfloat16)
            mixed_rows = jnp.einsum(
                "gqk,kgd->qgd", attn_probs, value_head, preferred_element_type=jnp.float32
            )
            return (mixed_rows, (top_score + jnp.log(row_total))[..., 0])

        mixed_heads, log_heads = lax.map(
            forward_one_head,
            (
                heads_first(seq_group(queries, block_index, group_size)),
                heads_first(key_part),
                heads_first(value_part),
            ),
        )
        return (heads_back(mixed_heads), jnp.moveaxis(log_heads, 0, 1))

    attended, log_totals = lax.map(forward_block, jnp.arange(block_count))
    attended_b = (
        ungroup(attended, row_count, seq_count)
        .reshape(token_count, local_width)
        .astype(jnp.bfloat16)
    )
    attention = lax.psum(jnp.dot(attended_b, out_full, preferred_element_type=jnp.float32), "tp")
    middle = start_flat + attention
    normed_mid = norm_rows(middle, gain_rows[1], offset_rows[1]).astype(jnp.bfloat16)
    expanded = jnp.dot(normed_mid, fc_full, preferred_element_type=jnp.float32)
    activated = gelu_tanh(expanded).astype(jnp.bfloat16)
    feedforward = lax.psum(
        jnp.dot(activated, proj_full, preferred_element_type=jnp.float32).astype(jnp.bfloat16), "tp"
    ).astype(jnp.float32)
    output = (middle + feedforward).astype(jnp.bfloat16).reshape(row_count, seq_count, model_width)
    grad_rows = out_grad.reshape(token_count, model_width)
    d_proj = jnp.einsum("nf,nd->fd", activated, grad_rows, preferred_element_type=jnp.float32)
    d_activated = jnp.einsum("nd,fd->nf", grad_rows, proj_full, preferred_element_type=jnp.float32)
    gelu_back = jax.vjp(gelu_tanh, expanded)[1]
    d_expanded = gelu_back(d_activated)[0].astype(jnp.bfloat16)
    d_fc = jnp.einsum("nd,nf->df", normed_mid, d_expanded, preferred_element_type=jnp.float32)
    d_normed_mid = lax.psum(
        jnp.einsum("nf,df->nd", d_expanded, fc_full, preferred_element_type=jnp.float32), "tp"
    )
    mid_back = jax.vjp(norm_rows, middle, gain_rows[1], offset_rows[1])[1]
    d_middle, d_gain_mid, d_offset_mid = mid_back(d_normed_mid)
    d_middle = d_middle + grad_rows.astype(jnp.float32)
    d_attention = d_middle.astype(jnp.bfloat16)
    d_out = jnp.einsum("nc,nd->cd", attended_b, d_attention, preferred_element_type=jnp.float32)
    d_attended = jnp.einsum("nd,cd->nc", d_attention, out_full, preferred_element_type=jnp.float32)
    d_attended = d_attended.astype(jnp.bfloat16).reshape(
        row_count, seq_count, local_heads, HEAD_DIM
    )

    def fetch_keys(block_index):
        whole_kv = lax.all_gather(
            seq_group(keys_values, block_index, group_size), "ctx", axis=0, tiled=True
        )
        return split_pairs(whole_kv, seq_length)

    def query_side(block_index, log_block):
        key_part, value_part = fetch_keys(block_index)
        query_seg = seq_group(seg_rows, block_index, group_size)
        key_seg = seq_group(seg_all, block_index, group_size)

        def query_one_head(five):
            query_head, key_head, value_head, grad_head, log_head = five
            return head_back(
                query_head,
                key_head,
                value_head,
                grad_head,
                log_head,
                row_places,
                key_places,
                query_seg,
                key_seg,
                score_scale,
            )

        return lax.map(
            query_one_head,
            (
                heads_first(seq_group(queries, block_index, group_size)),
                heads_first(key_part),
                heads_first(value_part),
                heads_first(seq_group(d_attended, block_index, group_size)),
                jnp.moveaxis(log_block, 1, 0),
            ),
        )

    def backward_block(block_pair):
        block_index, log_block = block_pair
        d_query, row_delta, d_keys, d_values = query_side(block_index, log_block)
        term = jnp.concatenate(
            [
                heads_back(d_keys).reshape(seq_length, group_size, local_width),
                heads_back(d_values).reshape(seq_length, group_size, local_width),
            ],
            axis=-1,
        )
        return (
            heads_back(d_query),
            lax.psum_scatter(
                term.astype(jnp.bfloat16), "ctx", scatter_dimension=0, tiled=True
            ).astype(jnp.float32),
        )

    d_queries, d_kv = lax.map(backward_block, (jnp.arange(block_count), log_totals))
    d_query_rows = ungroup(d_queries, row_count, seq_count).reshape(token_count, local_width)
    d_kv_rows = ungroup(d_kv, row_count, seq_count).reshape(token_count, 2 * local_width)
    d_projected = jnp.concatenate([d_query_rows, d_kv_rows], axis=1).astype(jnp.bfloat16)
    d_qkv = jnp.einsum("nd,nc->dc", normed, d_projected, preferred_element_type=jnp.float32)
    d_qkv = jnp.transpose(d_qkv.reshape(model_width, 3, local_width), (1, 0, 2))
    d_normed = lax.psum(
        jnp.einsum("nc,dc->nd", d_projected, qkv_matrix, preferred_element_type=jnp.float32).astype(
            jnp.bfloat16
        ),
        "tp",
    ).astype(jnp.float32)
    first_back = jax.vjp(norm_rows, start_flat, gain_rows[0], offset_rows[0])[1]
    d_start, d_gain_first, d_offset_first = first_back(d_normed)
    d_start_rows = (d_start + d_middle).reshape(row_count, seq_count, model_width)
    d_inputs = d_start_rows * keep_rows[:, :, None]
    d_thoughts = jnp.einsum("rts,rsd->tsd", select, d_start_rows, precision=PRECISE)
    d_gains = jnp.stack([d_gain_first, d_gain_mid])
    d_offsets = jnp.stack([d_offset_first, d_offset_mid])
    shares = (
        lax.psum_scatter(
            d_qkv.astype(jnp.bfloat16), "fsdp", scatter_dimension=1, tiled=True
        ).astype(jnp.float32),
        lax.psum_scatter(
            d_out.astype(jnp.bfloat16), "fsdp", scatter_dimension=1, tiled=True
        ).astype(jnp.float32),
        lax.psum_scatter(d_fc.astype(jnp.bfloat16), "fsdp", scatter_dimension=0, tiled=True).astype(
            jnp.float32
        ),
        lax.psum_scatter(
            d_proj.astype(jnp.bfloat16), "fsdp", scatter_dimension=1, tiled=True
        ).astype(jnp.float32),
        lax.psum_scatter(
            d_gains.astype(jnp.bfloat16), "fsdp", scatter_dimension=1, tiled=True
        ).astype(jnp.float32),
        lax.psum_scatter(
            d_offsets.astype(jnp.bfloat16), "fsdp", scatter_dimension=1, tiled=True
        ).astype(jnp.float32),
    )
    summed = (
        lax.psum(shares[0].astype(jnp.bfloat16), "ctx").astype(jnp.float32),
        lax.psum(shares[1].astype(jnp.bfloat16), "ctx").astype(jnp.float32),
        lax.psum(shares[2].astype(jnp.bfloat16), "ctx").astype(jnp.float32),
        lax.psum(shares[3].astype(jnp.bfloat16), "ctx").astype(jnp.float32),
        lax.psum(shares[4].astype(jnp.bfloat16), "ctx").astype(jnp.float32),
        lax.psum(shares[5].astype(jnp.bfloat16), "ctx").astype(jnp.float32),
        lax.psum(d_thoughts.astype(jnp.bfloat16), "ctx").astype(jnp.float32),
    )
    return (
        output,
        d_inputs,
        summed[6],
        summed[0],
        summed[1],
        summed[2],
        summed[3],
        summed[4],
        summed[5][0],
        summed[5][1],
    )


def solution(mesh):
    in_specs = (
        P("ctx", "fsdp", None),
        P(None, "fsdp", None),
        P(None, "fsdp"),
        P("fsdp", None),
        P(None, "fsdp", "tp"),
        P("tp", "fsdp"),
        P("fsdp", "tp"),
        P("tp", "fsdp"),
        P(None, "fsdp"),
        P(None, "fsdp"),
        P("ctx", "fsdp", None),
    )
    out_specs = (
        P("ctx", "fsdp", None),
        P("ctx", "fsdp", None),
        P(None, "fsdp", None),
        P(None, "fsdp", "tp"),
        P("tp", "fsdp"),
        P("fsdp", "tp"),
        P("tp", "fsdp"),
        P(None, "fsdp"),
        P("fsdp"),
        P("fsdp"),
    )
    return jax.shard_map(local, mesh=mesh, in_specs=in_specs, out_specs=out_specs, check_vma=False)
```

profile of v0, /device:TPU:0, one launch (start us, length us, event | category | flops | bytes accessed | tf_op | source)
XLA Modules:
  0.0 1466.0 jit_solution(1052572031871166158)
XLA Ops:
  8.1 6.3 all-gather
  23.3 13.1 all_gather.26
  71.5 123.2 %while.55 = (s32[]{:T(128)}, bf16[2,1024,1,3,64]{1,4,3,2,0:T(8,128)(2,1)}, f32[2,1,3,1024]{3,0,2,1:T(2,128)S(1)}, s32[2]{0:T(128)S(1)}, bf16[1024,2,3,64]{0,3,1,...) while((s32[]{:T(128)}, ...), condition=%wide.region_10.11_spmd.clone, body=%wide.region_5.10_spmd.clone.sunk | while | flops 559939584 | bytes 42727944 | solution.py:186
  76.1 27.9 %all-gather.11.cloned.1.call-done = bf16[2048,1,384]{0,2,1:T(8,128)(2,1)} async-done(((bf16[1024,1,384]{0,2,1:T(8,128)(2,1)}), bf16[2048,1,384]{0,2,1:T(8,128)(2,1)}) %all-gather.11.cloned.1.call-update) | async-done | bytes 1572880 | tf_op jit(solution)/shard_map/while/body/eval_jaxpr/all_gather | solution.py:155
  106.4 25.7 %while.58 = (s32[]{:T(128)}, bf16[3,1024,1,64]{1,3,2,0:T(8,128)(2,1)}, f32[3,1,1024]{2,1,0:T(1,128)S(1)}, bf16[3,2048,1,64]{1,3,2,0:T(8,128)(2,1)}, s32[1024]{0:...) while((s32[]{:T(128)}, ...), condition=%wide.region_9.9_spmd, body=%wide.region_6.8_spmd.sunk | while | flops 559938560 | bytes 29296816 | solution.py:176
  138.3 26.5 %all-gather.11.cloned.1.call-done = bf16[2048,1,384]{0,2,1:T(8,128)(2,1)} async-done(((bf16[1024,1,384]{0,2,1:T(8,128)(2,1)}), bf16[2048,1,384]{0,2,1:T(8,128)(2,1)}) %all-gather.11.cloned.1.call-update) | async-done | bytes 1572880 | tf_op jit(solution)/shard_map/while/body/eval_jaxpr/all_gather | solution.py:155
  167.2 25.7 %while.58 = (s32[]{:T(128)}, bf16[3,1024,1,64]{1,3,2,0:T(8,128)(2,1)}, f32[3,1,1024]{2,1,0:T(1,128)S(1)}, bf16[3,2048,1,64]{1,3,2,0:T(8,128)(2,1)}, s32[1024]{0:...) while((s32[]{:T(128)}, ...), condition=%wide.region_9.9_spmd, body=%wide.region_6.8_spmd.sunk | while | flops 559938560 | bytes 29296816 | solution.py:176
  203.7 8.7 all_gather.27
  217.5 10.3 copy.142
  227.8 7.7 reshape.379
  235.5 8.5 reshape.374
  244.1 7.5 fusion.95
  251.5 188.5 %all-reduce.8.cloned.1.call-done = f32[2048,768]{1,0:T(8,128)} async-done(((f32[2048,768]{1,0:T(8,128)}), f32[2048,768]{1,0:T(8,128)}) %all-reduce.8.cloned.1.call-update) | async-done | bytes 6291472 | tf_op jit(solution)/shard_map/psum | solution.py:192
  450.2 10.0 fusion.62
  466.5 8.1 reshape.398
  474.6 213.9 %all-reduce.10.cloned.1.call-done = f32[2048,768]{1,0:T(8,128)} async-done(((f32[2048,768]{1,0:T(8,128)}), f32[2048,768]{1,0:T(8,128)}) %all-reduce.10.cloned.1.call-update) | async-done | bytes 6291472 | tf_op jit(solution)/shard_map/psum | solution.py:207
  688.5 6.4 multiply_reduce_fusion.1
  715.9 280.1 %while.57 = (s32[]{:T(128)}, bf16[2,1024,1,3,64]{1,4,3,2,0:T(8,128)(2,1)}, bf16[2,1024,1,384]{1,3,2,0:T(8,128)(2,1)}, s32[2]{0:T(128)S(1)}, bf16[1024,2,3,64]{0,...) while((s32[]{:T(128)}, ...), condition=%wide.region_23.24_spmd.clone, body=%wide.region_18.23_spmd.clone.sunk | while | flops 1373175808 | bytes 154253136 | solution.py:274
  721.0 25.1 %all-gather.13.cloned.1.call-done = bf16[2048,1,384]{0,2,1:T(8,128)(2,1)} async-done(((bf16[1024,1,384]{0,2,1:T(8,128)(2,1)}), bf16[2048,1,384]{0,2,1:T(8,128)(2,1)}) %all-gather.13.cloned.1.call-update) | async-done | bytes 1572880 | tf_op jit(solution)/shard_map/while/body/eval_jaxpr/all_gather | solution.py:221
  748.7 75.5 %while.59 = (s32[]{:T(128)}, bf16[3,1024,1,64]{1,3,2,0:T(8,128)(2,1)}, bf16[3,2048,1,64]{1,3,2,0:T(8,128)(2,1)}, bf16[3,2048,1,64]{1,3,2,0:T(8,128)(2,1)}, bf16[...) while((s32[]{:T(128)}, ...), condition=%wide.region_21.21_spmd, body=%wide.region_19.20_spmd.sunk | while | flops 1369635840 | bytes 108578080 | solution.py:246
  751.0 7.2 multiply_reduce_fusion.6
  758.2 6.6 multiply_convert_fusion.5
  776.2 7.2 multiply_reduce_fusion.6
  783.3 6.6 multiply_convert_fusion.5
  801.3 7.2 multiply_reduce_fusion.6
  808.5 6.6 multiply_convert_fusion.5
  828.9 24.5 %reduce-scatter.28.cloned.1.call-done = bf16[1024,1,384]{0,2,1:T(8,128)(2,1)} async-done(((bf16[2048,1,384]{0,2,1:T(8,128)(2,1)}), bf16[1024,1,384]{0,2,1:T(8,128)(2,1)}) %reduce-scatter.28.cloned.1.call-update) | async-done | bytes 786448 | tf_op jit(solution)/shard_map/while/body/eval_jaxpr/reduce_scatter | solution.py:269
  860.4 26.1 %all-gather.13.cloned.1.call-done = bf16[2048,1,384]{0,2,1:T(8,128)(2,1)} async-done(((bf16[1024,1,384]{0,2,1:T(8,128)(2,1)}), bf16[2048,1,384]{0,2,1:T(8,128)(2,1)}) %all-gather.13.cloned.1.call-update) | async-done | bytes 1572880 | tf_op jit(solution)/shard_map/while/body/eval_jaxpr/all_gather | solution.py:221
  889.2 75.5 %while.59 = (s32[]{:T(128)}, bf16[3,1024,1,64]{1,3,2,0:T(8,128)(2,1)}, bf16[3,2048,1,64]{1,3,2,0:T(8,128)(2,1)}, bf16[3,2048,1,64]{1,3,2,0:T(8,128)(2,1)}, bf16[...) while((s32[]{:T(128)}, ...), condition=%wide.region_21.21_spmd, body=%wide.region_19.20_spmd.sunk | while | flops 1369635840 | bytes 108578080 | solution.py:246
  891.5 7.2 multiply_reduce_fusion.6
  898.6 6.6 multiply_convert_fusion.5
  916.6 7.2 multiply_reduce_fusion.6
  923.8 6.6 multiply_convert_fusion.5
  941.8 7.2 multiply_reduce_fusion.6
  949.0 6.6 multiply_convert_fusion.5
  969.4 24.5 %reduce-scatter.28.cloned.1.call-done = bf16[1024,1,384]{0,2,1:T(8,128)(2,1)} async-done(((bf16[2048,1,384]{0,2,1:T(8,128)(2,1)}), bf16[1024,1,384]{0,2,1:T(8,128)(2,1)}) %reduce-scatter.28.cloned.1.call-update) | async-done | bytes 786448 | tf_op jit(solution)/shard_map/while/body/eval_jaxpr/reduce_scatter | solution.py:269
  1023.2 6.6 convolution_convert_fusion.5
  1029.9 7.2 convolution_convert_fusion.4
  1038.8 8.6 reduce-scatter.20.cloned.1.call-done
  1049.6 26.3 %reduce-scatter.16.cloned.1.call-done = bf16[192,768]{1,0:T(8,128)(2,1)} async-done(((bf16[768,768]{1,0:T(8,128)(2,1)}), bf16[192,768]{1,0:T(8,128)(2,1)}) %reduce-scatter.16.cloned.1.call-update) | async-done | bytes 294928 | tf_op jit(solution)/shard_map/reduce_scatter | solution.py:300
  1075.9 28.2 %reduce-scatter.18.cloned.1.call-done = bf16[768,192]{0,1:T(8,128)(2,1)} async-done(((bf16[768,768]{0,1:T(8,128)(2,1)}), bf16[768,192]{0,1:T(8,128)(2,1)}) %reduce-scatter.18.cloned.1.call-update) | async-done | bytes 294928 | tf_op jit(solution)/shard_map/reduce_scatter | solution.py:303
  1104.2 8.7 convolution_convert_fusion.1
  1118.9 24.6 %all-reduce.14.cloned.1.call-done = (bf16[3,192,192]{1,2,0:T(8,128)(2,1)}, bf16[192,192]{1,0:T(8,128)(2,1)}, bf16[192,768]{1,0:T(8,128)(2,1)}, bf16[768,192]{0,1:T(8,128)(2,1)}) async-done(((bf16[3,192,192]{1,2,0:T(8,128)(2,1)}, bf16[192,192]{1,0:T(8,128)(2,1)}, bf16[192,768]{1,0:T(8,128)(2,1)}, bf16[768,192]{0,1:T(8,128)(2,1)}), (bf16[3,192,192]{1,2,0:T(8,128)(2,1)}, bf16[192,192]{1,0:T(8,128)(2,1)}, ...) | async-done | bytes 884752 | tf_op jit(solution)/shard_map/psum | solution.py:314
  1150.6 218.4 %all-reduce.12.cloned.1.call-done = (bf16[2048,768]{1,0:T(8,128)(2,1)}, bf16[2048,768]{1,0:T(8,128)(2,1)}) async-done(((bf16[2048,768]{1,0:T(8,128)(2,1)}, bf16[2048,768]{1,0:T(8,128)(2,1)}), (bf16[2048,768]{1,0:T(8,128)(2,1)}, bf16[2048,768]{1,0:T(8,128)(2,1)})) %all-reduce.12.cloned.1.call-update) | async-done | bytes 6291472 | tf_op jit(solution)/shard_map/psum | solution.py:280
  1391.4 8.2 reshape.381
  1415.0 10.3 copy.166
  1426.3 21.0 %reduce-scatter.26.cloned.1.call-done = bf16[192,2]{1,0:T(8,128)(2,1)} async-done(((bf16[768,2]{1,0:T(8,128)(2,1)}), bf16[192,2]{1,0:T(8,128)(2,1)}) %reduce-scatter.26.cloned.1.call-update) | async-done | bytes 784
  1448.1 8.4 all-reduce.1
  (446 shorter events, 337.8 us)
Async XLA Ops:
  8.0 30.5 %copy-start = (bf16[6,2,768]{2,1,0:T(2,128)(2,1)S(1)}, bf16[6,2,768]{2,1,0:T(2,128)(2,1)}, u32[]{:S(2)}) copy-start(bf16[6,2,768]{2,1,0:T(2,128)(2,1)} %param.20) | copy-start | bytes 55300
  8.0 34.2 %copy-start.37 = (s32[1024]{0:T(1024)}, s32[1024]{0:T(1024)S(1)}, u32[]{:S(2)}) copy-start(s32[1024]{0:T(1024)S(1)} %iota_add_fusion.2) | copy-start | bytes 12292
  15.0 29.2 %copy-start.35 = (f32[768]{0:T(1024)}, f32[768]{0:T(1024)S(1)}, u32[]{:S(2)}) copy-start(f32[768]{0:T(1024)S(1)} %get-tuple-element.553) | copy-start | bytes 9220
  22.0 20.2 %copy-start.31 = (f32[1024,2]{0,1:T(2,128)}, f32[1024,2]{0,1:T(2,128)S(1)}, u32[]{:S(2)}) copy-start(f32[1024,2]{0,1:T(2,128)S(1)} %broadcast_subtract_fusion) | copy-start | bytes 24580
  71.5 123.9 %copy-start.39 = (bf16[192,192]{1,0:T(8,128)(2,1)S(1)}, bf16[192,192]{1,0:T(8,128)(2,1)}, u32[]{:S(2)}) copy-start(bf16[192,192]{1,0:T(8,128)(2,1)} %param.24) | copy-start | bytes 221188
  71.7 32.3 %all-gather.11.cloned.1.call-start = ((), (), s32[]{:S(2)}) async-start(), calls=%async_computation.19 | async-start | bytes 2359296 | tf_op jit(solution)/shard_map/while/body/eval_jaxpr/all_gather | solution.py:155
  134.0 30.9 %all-gather.11.cloned.1.call-start = ((), (), s32[]{:S(2)}) async-start(), calls=%async_computation.19 | async-start | bytes 2359296 | tf_op jit(solution)/shard_map/while/body/eval_jaxpr/all_gather | solution.py:155
  194.8 49.3 %all-gather.9.cloned.1.call-start = ((), (), s32[]{:S(2)}) async-start(), calls=%async_computation.9 | async-start | bytes 1474560 | tf_op jit(solution)/shard_map/all_gather | solution.py:117
  195.4 244.6 %all-reduce.8.cloned.1.call-start = ((), (), s32[]{:S(2)}) async-start(), calls=%async_computation.7 | async-start | bytes 12582912 | tf_op jit(solution)/shard_map/psum | solution.py:192
  216.9 233.3 %all-gather.7.cloned.1.call-start = ((), (), s32[]{:S(2)}) async-start(), calls=%async_computation.8 | async-start | bytes 1474560 | tf_op jit(solution)/shard_map/all_gather | solution.py:116
  217.5 471.0 %all-reduce.10.cloned.1.call-start = ((), (), s32[]{:S(2)}) async-start(), calls=%async_computation.10 | async-start | bytes 12582912 | tf_op jit(solution)/shard_map/psum | solution.py:207
  450.2 11.8 copy-start.49
  703.4 12.5 copy-start.30
  716.0 32.7 %copy-start.5 = (bf16[1024,2,384]{0,2,1:T(8,128)(2,1)}, bf16[1024,2,384]{0,2,1:T(8,128)(2,1)S(1)}, u32[]{:S(2)}) copy-start(bf16[1024,2,384]{0,2,1:T(8,128)(2,1)S(1)} %get-tuple-element.1164) | copy-start | bytes 4718596 | tf_op jit(solution)/shard_map/while
  716.0 32.7 %copy-start.13 = (bf16[1024,2,3,64]{0,3,1,2:T(8,128)(2,1)}, bf16[1024,2,3,64]{0,3,1,2:T(8,128)(2,1)S(1)}, u32[]{:S(2)}) copy-start(bf16[1024,2,3,64]{0,3,1,2:T(8,128)(2,1)S(1)} %get-tuple-element.1163) | copy-start | bytes 2359300 | tf_op jit(solution)/shard_map/while
  716.0 30.0 %all-gather.13.cloned.1.call-start = ((), (), s32[]{:S(2)}) async-start(), calls=%async_computation.20 | async-start | bytes 2359296 | tf_op jit(solution)/shard_map/while/body/eval_jaxpr/all_gather | solution.py:221
  719.7 133.6 %reduce-scatter.28.cloned.1.call-start = ((), (), s32[]{:S(2)}) async-start(), calls=%async_computation.21 | async-start | bytes 2359296 | tf_op jit(solution)/shard_map/while/body/eval_jaxpr/reduce_scatter | solution.py:269
  764.8 7.4 copy-start.16
  789.9 7.4 copy-start.16
  815.1 7.4 copy-start.16
  824.3 31.2 %copy-start.6 = (bf16[1024,2,384]{0,2,1:T(8,128)(2,1)S(1)}, bf16[1024,2,384]{0,2,1:T(8,128)(2,1)}, u32[]{:S(2)}) copy-start(bf16[1024,2,384]{0,2,1:T(8,128)(2,1)} %copy-done.5) | copy-start | bytes 4718596 | tf_op jit(solution)/shard_map/while
  824.3 31.2 %copy-start.14 = (bf16[1024,2,3,64]{0,3,1,2:T(8,128)(2,1)S(1)}, bf16[1024,2,3,64]{0,3,1,2:T(8,128)(2,1)}, u32[]{:S(2)}) copy-start(bf16[1024,2,3,64]{0,3,1,2:T(8,128)(2,1)} %copy-done.13) | copy-start | bytes 2359300 | tf_op jit(solution)/shard_map/while
  855.4 33.8 %copy-start.5 = (bf16[1024,2,384]{0,2,1:T(8,128)(2,1)}, bf16[1024,2,384]{0,2,1:T(8,128)(2,1)S(1)}, u32[]{:S(2)}) copy-start(bf16[1024,2,384]{0,2,1:T(8,128)(2,1)S(1)} %get-tuple-element.1164) | copy-start | bytes 4718596 | tf_op jit(solution)/shard_map/while
  855.4 33.8 %copy-start.13 = (bf16[1024,2,3,64]{0,3,1,2:T(8,128)(2,1)}, bf16[1024,2,3,64]{0,3,1,2:T(8,128)(2,1)S(1)}, u32[]{:S(2)}) copy-start(bf16[1024,2,3,64]{0,3,1,2:T(8,128)(2,1)S(1)} %get-tuple-element.1163) | copy-start | bytes 2359300 | tf_op jit(solution)/shard_map/while
  855.4 31.1 %all-gather.13.cloned.1.call-start = ((), (), s32[]{:S(2)}) async-start(), calls=%async_computation.20 | async-start | bytes 2359296 | tf_op jit(solution)/shard_map/while/body/eval_jaxpr/all_gather | solution.py:221
  859.1 134.7 %reduce-scatter.28.cloned.1.call-start = ((), (), s32[]{:S(2)}) async-start(), calls=%async_computation.21 | async-start | bytes 2359296 | tf_op jit(solution)/shard_map/while/body/eval_jaxpr/reduce_scatter | solution.py:269
  905.2 7.4 copy-start.16
  955.5 7.4 copy-start.16
  964.7 31.2 %copy-start.6 = (bf16[1024,2,384]{0,2,1:T(8,128)(2,1)S(1)}, bf16[1024,2,384]{0,2,1:T(8,128)(2,1)}, u32[]{:S(2)}) copy-start(bf16[1024,2,384]{0,2,1:T(8,128)(2,1)} %copy-done.5) | copy-start | bytes 4718596 | tf_op jit(solution)/shard_map/while
  964.7 31.2 %copy-start.14 = (bf16[1024,2,3,64]{0,3,1,2:T(8,128)(2,1)S(1)}, bf16[1024,2,3,64]{0,3,1,2:T(8,128)(2,1)}, u32[]{:S(2)}) copy-start(bf16[1024,2,3,64]{0,3,1,2:T(8,128)(2,1)} %copy-done.13) | copy-start | bytes 2359300 | tf_op jit(solution)/shard_map/while
  995.9 41.3 %reduce-scatter.22.cloned.1.call-start = ((), (), s32[]{:S(2)}) async-start(), calls=%async_computation.14 | async-start | bytes 491520
  996.5 51.0 %reduce-scatter.20.cloned.1.call-start = ((), (), s32[]{:S(2)}) async-start(), calls=%async_computation.13 | async-start | bytes 1228800
  1018.7 11.2 copy-start.10
  1023.0 52.9 %reduce-scatter.16.cloned.1.call-start = ((), (), s32[]{:S(2)}) async-start(), calls=%async_computation.11 | async-start | bytes 1474560 | tf_op jit(solution)/shard_map/reduce_scatter | solution.py:300
  1029.8 74.3 %reduce-scatter.18.cloned.1.call-start = ((), (), s32[]{:S(2)}) async-start(), calls=%async_computation.12 | async-start | bytes 1474560 | tf_op jit(solution)/shard_map/reduce_scatter | solution.py:303
  1037.1 106.3 %all-reduce.14.cloned.1.call-start = ((), (), s32[]{:S(2)}) async-start(), calls=%async_computation.18 | async-start | bytes 1966080 | tf_op jit(solution)/shard_map/psum | solution.py:314
  1104.2 8.8 copy-start.23
  1104.2 8.8 copy-start.24
  1104.2 8.8 copy-start.28
  1104.2 264.8 %all-reduce.12.cloned.1.call-start = ((), (), s32[]{:S(2)}) async-start(), calls=%async_computation.17 | async-start | bytes 12582912 | tf_op jit(solution)/shard_map/psum | solution.py:280
  1117.2 308.2 %reduce-scatter.24.cloned.1.call-start = ((), (), s32[]{:S(2)}) async-start(), calls=%async_computation.15 | async-start | bytes 245760
  1369.0 8.6 copy-start.36
  1377.6 9.2 slice-start.2
  1391.4 8.2 copy-start.32
  1399.6 7.9 copy-start.38
  1399.6 7.9 copy-start.44
  1406.4 40.9 %reduce-scatter.26.cloned.1.call-start = ((), (), s32[]{:S(2)}) async-start(), calls=%async_computation.16 | async-start | bytes 245760
  1412.3 46.0 %copy-start.1 = (bf16[6,2,768]{2,1,0:T(2,128)(2,1)S(1)}, bf16[6,2,768]{2,1,0:T(2,128)(2,1)}, u32[]{:S(2)}) copy-start(bf16[6,2,768]{2,1,0:T(2,128)(2,1)} %param.20) | copy-start | bytes 55300
  (64 other events, 202.9 us)
Sparse Core Ops, SparseCore 0:
  75.4 28.5 all-gather.10
  137.6 27.1 all-gather.10
  217.0 222.9 all-reduce.7
  466.7 221.7 all-reduce.9
  719.8 26.1 all-gather.12
  827.2 26.0 reduce-scatter.27
  859.3 27.1 all-gather.12
  967.7 26.0 reduce-scatter.27
  1104.3 39.1 all-reduce.13
  1145.7 223.2 all-reduce.11
Sparse Core Ops, SparseCore 1:
  196.8 19.4 all-gather.8
  218.9 17.4 all-gather.6
  999.5 20.7 reduce-scatter.21
  1023.0 24.4 reduce-scatter.19
  1050.3 25.6 reduce-scatter.15
  1078.5 25.6 reduce-scatter.17
  1406.4 18.7 reduce-scatter.23
  1427.5 19.7 reduce-scatter.25
where the time goes:
time: 1480 us; the launch traced here: 1470 us
  waiting for transfers between devices  886 us (60%)
  matrix products  218 us (15%)
  local copies, waits for them, and re-layouts  176 us (12%)
  other arithmetic  116 us (8%)
  blocking collectives  42.1 us (3%)
  between operations  16.5 us (1%)
    psum x1, waiting for transfers between devices, local(): lax.psum(jnp.einsum('nc,dc->nd', d_projected, qkv_matrix, preferred_eleme...  218 us
    psum x1, waiting for transfers between devices, local(): lax.psum(jnp.einsum('nf,df->nd', d_expanded, fc_full, preferred_element_t...  214 us
    psum x1, waiting for transfers between devices, local(): lax.psum(jnp.dot(attended_b, out_full, preferred_element_type=jnp.float32...  188 us
    dot_general x12, matrix products, score_head(): jnp.einsum('qgd,kgd->gqk', query_head, key_head, preferred_element_type=j...  62.1 us
    all_gather x2, waiting for transfers between devices, forward_block(): lax.all_gather(seq_group(keys_values, block_index, group_size), 'ctx', ax...  54.4 us
    all_gather x2, waiting for transfers between devices, fetch_keys(): lax.all_gather(seq_group(keys_values, block_index, group_size), 'ctx', ax...  51.2 us
    reduce_scatter x2, waiting for transfers between devices, backward_block(): lax.psum_scatter(term.astype(jnp.bfloat16), 'ctx', scatter_dimension=0, t...  48.9 us
    unnamed x106, local copies, waits for them, and re-layouts  48.5 us
  transfers between devices with their start and end apart: 18, of which 14 were waited for; matrix products, arithmetic and copies ran while one was open for 11% of the time, Pallas kernels for 0%

commit v1 on v0

--- a/solution.py
+++ b/solution.py
@@ -7,6 +7,23 @@
 EPSILON = 1e-05
 NEGATIVE = -1000000000.0
 PRECISE = lax.Precision.HIGHEST
+
+
+def in_order(parts, dim):
+    parts = jnp.moveaxis(parts, 0, dim)
+    shape = parts.shape
+    return parts.reshape(*shape[:dim], shape[dim] * shape[dim + 1], *shape[dim + 2 :])
+
+
+def doubled(shard, axis):
+    length, mine = (lax.axis_size(axis), lax.axis_index(axis))
+    parts, bit = (shard[None], 1)
+    while bit < length:
+        theirs = lax.ppermute(parts, axis, [(i, i ^ bit) for i in range(length)])
+        low = mine & bit == 0
+        parts = jnp.concatenate([jnp.where(low, parts, theirs), jnp.where(low, theirs, parts)])
+        bit *= 2
+    return parts
 
 
 def norm_rows(values, gain_row, offset):
@@ -152,9 +169,8 @@
         return (key_part, value_part)
 
     def forward_block(block_index):
-        whole_kv = lax.all_gather(
-            seq_group(keys_values, block_index, group_size), "ctx", axis=0, tiled=True
-        )
+        x = seq_group(keys_values, block_index, group_size)
+        whole_kv = in_order(doubled(x, "ctx"), 0)
         key_part, value_part = split_pairs(whole_kv, seq_length)
         query_seg = seq_group(seg_rows, block_index, group_size)
         key_seg = seq_group(seg_all, block_index, group_size)

time: 1480 us -> 1460 us (0.986)
  waiting for transfers between devices: 886 us -> 866 us
    all_gather x2 -> x0, waiting for transfers between devices: 54.4 us -> none  [forward_block(): lax.all_gather(seq_group(keys_values, block_index, group_size), 'ctx', ax...]
    ppermute x0 -> x2, waiting for transfers between devices: none -> 36.3 us  [doubled(): theirs = lax.ppermute(parts, axis, [(i, i ^ bit) for i in range(length)])]
    unnamed x106 -> x109, local copies, waits for them, and re-layouts: 48.5 us -> 48 us
  transfers between devices with their start and end apart: 18 -> 18, of which waited for: 14 -> 14; matrix products, arithmetic and copies ran while one was open for 11% -> 17% of each run, Pallas kernels for 0% -> 0%
where the time goes in v1:
time: 1460 us; the launch traced here: 1450 us
  waiting for transfers between devices  866 us (59%)
  matrix products  217 us (15%)
  local copies, waits for them, and re-layouts  175 us (12%)
  other arithmetic  120 us (8%)
  blocking collectives  40.8 us (3%)
  between operations  16.8 us (1%)
    psum x1, waiting for transfers between devices, local(): lax.psum(jnp.einsum('nc,dc->nd', d_projected, qkv_matrix, preferred_eleme...  219 us
    psum x1, waiting for transfers between devices, local(): lax.psum(jnp.einsum('nf,df->nd', d_expanded, fc_full, preferred_element_t...  209 us
    psum x1, waiting for transfers between devices, local(): lax.psum(jnp.dot(attended_b, out_full, preferred_element_type=jnp.float32...  190 us
    dot_general x12, matrix products, score_head(): jnp.einsum('qgd,kgd->gqk', query_head, key_head, preferred_element_type=j...  62.5 us
    all_gather x2, waiting for transfers between devices, fetch_keys(): lax.all_gather(seq_group(keys_values, block_index, group_size), 'ctx', ax...  51.2 us
    reduce_scatter x2, waiting for transfers between devices, backward_block(): lax.psum_scatter(term.astype(jnp.bfloat16), 'ctx', scatter_dimension=0, t...  48.9 us
    unnamed x109, local copies, waits for them, and re-layouts  48 us
    convert_element_type x6, other arithmetic, head_back(): (attn_probs * (d_probs - row_delta[..., None])).astype(jnp.bfloat16)  39.3 us
  transfers between devices with their start and end apart: 18, of which 14 were waited for; matrix products, arithmetic and copies ran while one was open for 17% of the time, Pallas kernels for 0%

profile of v1, /device:TPU:0, one launch (start us, length us, event | category | flops | bytes accessed | tf_op | source)
XLA Modules:
  0.0 1447.8 jit_solution(6269633003471216985)
XLA Ops:
  8.8 6.3 all-gather
  24.0 14.5 all_gather.23
  69.9 111.5 %while.55 = (s32[]{:T(128)}, bf16[2,1024,1,3,64]{1,4,3,2,0:T(8,128)(2,1)}, f32[2,1,3,1024]{3,0,2,1:T(2,128)S(1)}, s32[2]{0:T(128)S(1)}, bf16[1024,2,3,64]{0,3,1,...) while((s32[]{:T(128)}, ...), condition=%wide.region_10.11_spmd.clone, body=%wide.region_5.10_spmd.clone.sunk | while | flops 561512448 | bytes 60816008 | solution.py:202
  75.3 18.5 %collective-permute-done = bf16[1,1024,1,384]{3,1,2,0:T(8,128)(2,1)} collective-permute-done((bf16[1,1024,1,384]{3,1,2,0:T(8,128)(2,1)}, bf16[1,1024,1,384]{3,1,2,0:T(8,128)(2,1)}, u32[]{:S(2)}, u32[]{:S(2)}) %collective-permute-start) | collective-permute-done | bytes 786464 | tf_op jit(solution)/shard_map/while/body/eval_jaxpr/ppermute | solution.py:22
  98.4 25.9 %while.58 = (s32[]{:T(128)}, bf16[3,1024,1,64]{1,3,2,0:T(8,128)(2,1)}, f32[3,1,1024]{2,1,0:T(1,128)S(1)}, bf16[3,2048,1,64]{1,3,2,0:T(8,128)(2,1)}, s32[1024]{0:...) while((s32[]{:T(128)}, ...), condition=%wide.region_9.9_spmd, body=%wide.region_6.8_spmd.sunk | while | flops 559938560 | bytes 29296816 | solution.py:192
  131.3 17.7 %collective-permute-done = bf16[1,1024,1,384]{3,1,2,0:T(8,128)(2,1)} collective-permute-done((bf16[1,1024,1,384]{3,1,2,0:T(8,128)(2,1)}, bf16[1,1024,1,384]{3,1,2,0:T(8,128)(2,1)}, u32[]{:S(2)}, u32[]{:S(2)}) %collective-permute-start) | collective-permute-done | bytes 786464 | tf_op jit(solution)/shard_map/while/body/eval_jaxpr/ppermute | solution.py:22
  153.6 25.9 %while.58 = (s32[]{:T(128)}, bf16[3,1024,1,64]{1,3,2,0:T(8,128)(2,1)}, f32[3,1,1024]{2,1,0:T(1,128)S(1)}, bf16[3,2048,1,64]{1,3,2,0:T(8,128)(2,1)}, s32[1024]{0:...) while((s32[]{:T(128)}, ...), condition=%wide.region_9.9_spmd, body=%wide.region_6.8_spmd.sunk | while | flops 559938560 | bytes 29296816 | solution.py:192
  186.9 6.1 all_gather.24
  199.5 10.3 copy.150
  209.8 6.8 reshape.382
  216.6 9.3 reshape.377
  231.7 190.0 %all-reduce.8.cloned.1.call-done = f32[2048,768]{1,0:T(8,128)} async-done(((f32[2048,768]{1,0:T(8,128)}), f32[2048,768]{1,0:T(8,128)}) %all-reduce.8.cloned.1.call-update) | async-done | bytes 6291472 | tf_op jit(solution)/shard_map/psum | solution.py:208
  432.0 10.1 fusion.62
  448.4 7.6 reshape.402
  461.0 209.1 %all-reduce.10.cloned.1.call-done = f32[2048,768]{1,0:T(8,128)} async-done(((f32[2048,768]{1,0:T(8,128)}), f32[2048,768]{1,0:T(8,128)}) %all-reduce.10.cloned.1.call-update) | async-done | bytes 6291472 | tf_op jit(solution)/shard_map/psum | solution.py:223
  670.1 6.6 multiply_reduce_fusion.1
  694.3 281.7 %while.57 = (s32[]{:T(128)}, bf16[2,1024,1,3,64]{1,4,3,2,0:T(8,128)(2,1)}, bf16[2,1024,1,384]{1,3,2,0:T(8,128)(2,1)}, s32[2]{0:T(128)S(1)}, bf16[1024,2,3,64]{0,...) while((s32[]{:T(128)}, ...), condition=%wide.region_23.24_spmd.clone, body=%wide.region_18.23_spmd.clone.sunk | while | flops 1373175808 | bytes 141670160 | solution.py:290
  700.2 25.1 %all-gather.10.cloned.1.call-done = bf16[2048,1,384]{0,2,1:T(8,128)(2,1)} async-done(((bf16[1024,1,384]{0,2,1:T(8,128)(2,1)}), bf16[2048,1,384]{0,2,1:T(8,128)(2,1)}) %all-gather.10.cloned.1.call-update) | async-done | bytes 1572880 | tf_op jit(solution)/shard_map/while/body/eval_jaxpr/all_gather | solution.py:237
  728.0 75.5 %while.59 = (s32[]{:T(128)}, bf16[3,1024,1,64]{1,3,2,0:T(8,128)(2,1)}, bf16[3,2048,1,64]{1,3,2,0:T(8,128)(2,1)}, bf16[3,2048,1,64]{1,3,2,0:T(8,128)(2,1)}, bf16[...) while((s32[]{:T(128)}, ...), condition=%wide.region_21.21_spmd, body=%wide.region_19.20_spmd.sunk | while | flops 1369635840 | bytes 108578080 | solution.py:262
  730.3 7.2 multiply_reduce_fusion.6
  737.4 6.6 multiply_convert_fusion.5
  755.4 7.2 multiply_reduce_fusion.6
  762.6 6.6 multiply_convert_fusion.5
  780.6 7.2 multiply_reduce_fusion.6
  787.8 6.6 multiply_convert_fusion.5
  808.1 24.4 %reduce-scatter.28.cloned.1.call-done = bf16[1024,1,384]{0,2,1:T(8,128)(2,1)} async-done(((bf16[2048,1,384]{0,2,1:T(8,128)(2,1)}), bf16[1024,1,384]{0,2,1:T(8,128)(2,1)}) %reduce-scatter.28.cloned.1.call-update) | async-done | bytes 786448 | tf_op jit(solution)/shard_map/while/body/eval_jaxpr/reduce_scatter | solution.py:285
  840.6 26.1 %all-gather.10.cloned.1.call-done = bf16[2048,1,384]{0,2,1:T(8,128)(2,1)} async-done(((bf16[1024,1,384]{0,2,1:T(8,128)(2,1)}), bf16[2048,1,384]{0,2,1:T(8,128)(2,1)}) %all-gather.10.cloned.1.call-update) | async-done | bytes 1572880 | tf_op jit(solution)/shard_map/while/body/eval_jaxpr/all_gather | solution.py:237
  869.4 75.5 %while.59 = (s32[]{:T(128)}, bf16[3,1024,1,64]{1,3,2,0:T(8,128)(2,1)}, bf16[3,2048,1,64]{1,3,2,0:T(8,128)(2,1)}, bf16[3,2048,1,64]{1,3,2,0:T(8,128)(2,1)}, bf16[...) while((s32[]{:T(128)}, ...), condition=%wide.region_21.21_spmd, body=%wide.region_19.20_spmd.sunk | while | flops 1369635840 | bytes 108578080 | solution.py:262
  871.7 7.2 multiply_reduce_fusion.6
  878.8 6.6 multiply_convert_fusion.5
  896.8 7.2 multiply_reduce_fusion.6
  904.0 6.6 multiply_convert_fusion.5
  922.0 7.2 multiply_reduce_fusion.6
  929.1 6.6 multiply_convert_fusion.5
  949.5 24.5 %reduce-scatter.28.cloned.1.call-done = bf16[1024,1,384]{0,2,1:T(8,128)(2,1)} async-done(((bf16[2048,1,384]{0,2,1:T(8,128)(2,1)}), bf16[1024,1,384]{0,2,1:T(8,128)(2,1)}) %reduce-scatter.28.cloned.1.call-update) | async-done | bytes 786448 | tf_op jit(solution)/shard_map/while/body/eval_jaxpr/reduce_scatter | solution.py:285
  1003.7 6.6 convolution_convert_fusion.5
  1010.3 7.2 convolution_convert_fusion.4
  1019.5 8.8 reduce-scatter.20.cloned.1.call-done
  1030.4 26.4 %reduce-scatter.16.cloned.1.call-done = bf16[192,768]{1,0:T(8,128)(2,1)} async-done(((bf16[768,768]{1,0:T(8,128)(2,1)}), bf16[192,768]{1,0:T(8,128)(2,1)}) %reduce-scatter.16.cloned.1.call-update) | async-done | bytes 294928 | tf_op jit(solution)/shard_map/reduce_scatter | solution.py:316
  1056.8 28.7 %reduce-scatter.18.cloned.1.call-done = bf16[768,192]{0,1:T(8,128)(2,1)} async-done(((bf16[768,768]{0,1:T(8,128)(2,1)}), bf16[768,192]{0,1:T(8,128)(2,1)}) %reduce-scatter.18.cloned.1.call-update) | async-done | bytes 294928 | tf_op jit(solution)/shard_map/reduce_scatter | solution.py:319
  1085.6 8.8 convolution_convert_fusion.1
  1100.3 24.2 %all-reduce.14.cloned.1.call-done = (bf16[3,192,192]{1,2,0:T(8,128)(2,1)}, bf16[192,192]{1,0:T(8,128)(2,1)}, bf16[192,768]{1,0:T(8,128)(2,1)}, bf16[768,192]{0,1:T(8,128)(2,1)}) async-done(((bf16[3,192,192]{1,2,0:T(8,128)(2,1)}, bf16[192,192]{1,0:T(8,128)(2,1)}, bf16[192,768]{1,0:T(8,128)(2,1)}, bf16[768,192]{0,1:T(8,128)(2,1)}), (bf16[3,192,192]{1,2,0:T(8,128)(2,1)}, bf16[192,192]{1,0:T(8,128)(2,1)}, ...) | async-done | bytes 884752 | tf_op jit(solution)/shard_map/psum | solution.py:330
  1131.7 218.9 %all-reduce.12.cloned.1.call-done = (bf16[2048,768]{1,0:T(8,128)(2,1)}, bf16[2048,768]{1,0:T(8,128)(2,1)}) async-done(((bf16[2048,768]{1,0:T(8,128)(2,1)}, bf16[2048,768]{1,0:T(8,128)(2,1)}), (bf16[2048,768]{1,0:T(8,128)(2,1)}, bf16[2048,768]{1,0:T(8,128)(2,1)})) %all-reduce.12.cloned.1.call-update) | async-done | bytes 6291472 | tf_op jit(solution)/shard_map/psum | solution.py:296
  1350.6 6.1 add_convert_fusion
  1373.0 8.2 reshape.384
  1396.7 10.3 copy.174
  1407.9 21.0 %reduce-scatter.26.cloned.1.call-done = bf16[192,2]{1,0:T(8,128)(2,1)} async-done(((bf16[768,2]{1,0:T(8,128)(2,1)}), bf16[192,2]{1,0:T(8,128)(2,1)}) %reduce-scatter.26.cloned.1.call-update) | async-done | bytes 784
  1429.7 8.4 all-reduce.1
  (455 shorter events, 343.2 us)
Async XLA Ops:
  8.0 32.5 %copy-start = (bf16[6,2,768]{2,1,0:T(2,128)(2,1)S(1)}, bf16[6,2,768]{2,1,0:T(2,128)(2,1)}, u32[]{:S(2)}) copy-start(bf16[6,2,768]{2,1,0:T(2,128)(2,1)} %param.20) | copy-start | bytes 55300
  8.0 217.9 %all-gather.8.cloned.1.call-start = ((), (), s32[]{:S(2)}) async-start(), calls=%async_computation.9 | async-start | bytes 1474560 | tf_op jit(solution)/shard_map/all_gather | solution.py:134
  8.8 413.0 %all-reduce.8.cloned.1.call-start = ((), (), s32[]{:S(2)}) async-start(), calls=%async_computation.7 | async-start | bytes 12582912 | tf_op jit(solution)/shard_map/psum | solution.py:208
  8.8 35.5 %copy-start.38 = (s32[1024]{0:T(1024)}, s32[1024]{0:T(1024)S(1)}, u32[]{:S(2)}) copy-start(s32[1024]{0:T(1024)S(1)} %iota_add_fusion.2) | copy-start | bytes 12292
  15.8 30.6 %copy-start.36 = (f32[768]{0:T(1024)}, f32[768]{0:T(1024)S(1)}, u32[]{:S(2)}) copy-start(f32[768]{0:T(1024)S(1)} %get-tuple-element.553) | copy-start | bytes 9220
  22.8 21.5 %copy-start.32 = (f32[1024,2]{0,1:T(2,128)}, f32[1024,2]{0,1:T(2,128)S(1)}, u32[]{:S(2)}) copy-start(f32[1024,2]{0,1:T(2,128)S(1)} %broadcast_subtract_fusion) | copy-start | bytes 24580
  51.4 7.4 copy-start.12
  69.9 117.0 %copy-start.31 = (bf16[192,192]{0,1:T(8,128)(2,1)S(1)}, bf16[192,192]{0,1:T(8,128)(2,1)}, u32[]{:S(2)}) copy-start(bf16[192,192]{0,1:T(8,128)(2,1)} %copy.162) | copy-start | bytes 221188
  70.1 25.3 %copy-start.5 = (bf16[1024,2,384]{2,0,1:T(8,128)(2,1)}, bf16[1024,2,384]{2,0,1:T(8,128)(2,1)S(1)}, u32[]{:S(2)}) copy-start(bf16[1024,2,384]{2,0,1:T(8,128)(2,1)S(1)} %get-tuple-element.1131) | copy-start | bytes 4718596 | tf_op jit(solution)/shard_map/while
  73.7 20.1 %collective-permute-start = (bf16[1,1024,1,384]{3,1,2,0:T(8,128)(2,1)}, bf16[1,1024,1,384]{3,1,2,0:T(8,128)(2,1)}, u32[]{:S(2)}, u32[]{:S(2)}) collective-permute-start(bf16[1,1024,1,384]{3,1,2,0:T(8,128)(2,1)} %dynamic-slice_bitcast_fusion.9), channel_id=1, source_target_pairs={{0,4},{4,0},{1,5},{5,1},{2,6},{6,2},{3,7},{7,3},{8,12},{12,8},{9,1... | collective-permute-start | bytes 2359304 | tf_op jit(solution)/shard_map/while/body/eval_jaxpr/ppermute | solution.py:22
  98.4 27.7 %copy-start.6 = (bf16[1024,2,384]{2,0,1:T(8,128)(2,1)S(1)}, bf16[1024,2,384]{2,0,1:T(8,128)(2,1)}, u32[]{:S(2)}) copy-start(bf16[1024,2,384]{2,0,1:T(8,128)(2,1)} %copy-done.5) | copy-start | bytes 4718596 | tf_op jit(solution)/shard_map/while
  126.1 24.4 %copy-start.5 = (bf16[1024,2,384]{2,0,1:T(8,128)(2,1)}, bf16[1024,2,384]{2,0,1:T(8,128)(2,1)S(1)}, u32[]{:S(2)}) copy-start(bf16[1024,2,384]{2,0,1:T(8,128)(2,1)S(1)} %get-tuple-element.1131) | copy-start | bytes 4718596 | tf_op jit(solution)/shard_map/while
  129.7 19.3 %collective-permute-start = (bf16[1,1024,1,384]{3,1,2,0:T(8,128)(2,1)}, bf16[1,1024,1,384]{3,1,2,0:T(8,128)(2,1)}, u32[]{:S(2)}, u32[]{:S(2)}) collective-permute-start(bf16[1,1024,1,384]{3,1,2,0:T(8,128)(2,1)} %dynamic-slice_bitcast_fusion.9), channel_id=1, source_target_pairs={{0,4},{4,0},{1,5},{5,1},{2,6},{6,2},{3,7},{7,3},{8,12},{12,8},{9,1... | collective-permute-start | bytes 2359304 | tf_op jit(solution)/shard_map/while/body/eval_jaxpr/ppermute | solution.py:22
  153.6 27.8 %copy-start.6 = (bf16[1024,2,384]{2,0,1:T(8,128)(2,1)S(1)}, bf16[1024,2,384]{2,0,1:T(8,128)(2,1)}, u32[]{:S(2)}) copy-start(bf16[1024,2,384]{2,0,1:T(8,128)(2,1)} %copy-done.5) | copy-start | bytes 4718596 | tf_op jit(solution)/shard_map/while
  181.4 17.3 %copy-start.13 = (bf16[1024,2,3,64]{0,3,1,2:T(8,128)(2,1)}, bf16[1024,2,3,64]{0,3,1,2:T(8,128)(2,1)S(1)}, u32[]{:S(2)}) copy-start(bf16[1024,2,3,64]{0,3,1,2:T(8,128)(2,1)S(1)} %get-tuple-element.1219) | copy-start | bytes 2359300
  198.7 233.3 %all-gather.6.cloned.1.call-start = ((), (), s32[]{:S(2)}) async-start(), calls=%async_computation.8 | async-start | bytes 1474560 | tf_op jit(solution)/shard_map/all_gather | solution.py:133
  199.5 470.7 %all-reduce.10.cloned.1.call-start = ((), (), s32[]{:S(2)}) async-start(), calls=%async_computation.10 | async-start | bytes 12582912 | tf_op jit(solution)/shard_map/psum | solution.py:223
  216.6 464.3 %copy-start.9 = (bf16[2048,768]{1,0:T(8,128)(2,1)}, bf16[2048,768]{1,0:T(8,128)(2,1)S(1)}, u32[]{:S(2)}) copy-start(bf16[2048,768]{1,0:T(8,128)(2,1)S(1)} %reshape.382) | copy-start | bytes 9437188
  432.0 11.9 copy-start.50
  694.3 33.7 %copy-start.22 = (bf16[1024,2,3,64]{0,3,1,2:T(8,128)(2,1)}, bf16[1024,2,3,64]{0,3,1,2:T(8,128)(2,1)S(1)}, u32[]{:S(2)}) copy-start(bf16[1024,2,3,64]{0,3,1,2:T(8,128)(2,1)S(1)} %get-tuple-element.1177) | copy-start | bytes 2359300 | tf_op jit(solution)/shard_map/while
  694.3 31.0 %all-gather.10.cloned.1.call-start = ((), (), s32[]{:S(2)}) async-start(), calls=%async_computation.19 | async-start | bytes 2359296 | tf_op jit(solution)/shard_map/while/body/eval_jaxpr/all_gather | solution.py:237
  699.0 133.6 %reduce-scatter.28.cloned.1.call-start = ((), (), s32[]{:S(2)}) async-start(), calls=%async_computation.20 | async-start | bytes 2359296 | tf_op jit(solution)/shard_map/while/body/eval_jaxpr/reduce_scatter | solution.py:285
  794.3 7.4 copy-start.15
  803.5 31.1 %copy-start.23 = (bf16[1024,2,3,64]{0,3,1,2:T(8,128)(2,1)S(1)}, bf16[1024,2,3,64]{0,3,1,2:T(8,128)(2,1)}, u32[]{:S(2)}) copy-start(bf16[1024,2,3,64]{0,3,1,2:T(8,128)(2,1)} %copy-done.22) | copy-start | bytes 2359300 | tf_op jit(solution)/shard_map/while
  834.6 34.8 %copy-start.22 = (bf16[1024,2,3,64]{0,3,1,2:T(8,128)(2,1)}, bf16[1024,2,3,64]{0,3,1,2:T(8,128)(2,1)S(1)}, u32[]{:S(2)}) copy-start(bf16[1024,2,3,64]{0,3,1,2:T(8,128)(2,1)S(1)} %get-tuple-element.1177) | copy-start | bytes 2359300 | tf_op jit(solution)/shard_map/while
  834.6 32.1 %all-gather.10.cloned.1.call-start = ((), (), s32[]{:S(2)}) async-start(), calls=%async_computation.19 | async-start | bytes 2359296 | tf_op jit(solution)/shard_map/while/body/eval_jaxpr/all_gather | solution.py:237
  839.3 134.6 %reduce-scatter.28.cloned.1.call-start = ((), (), s32[]{:S(2)}) async-start(), calls=%async_computation.20 | async-start | bytes 2359296 | tf_op jit(solution)/shard_map/while/body/eval_jaxpr/reduce_scatter | solution.py:285
  910.6 7.4 copy-start.15
  935.7 7.4 copy-start.15
  944.9 31.1 %copy-start.23 = (bf16[1024,2,3,64]{0,3,1,2:T(8,128)(2,1)S(1)}, bf16[1024,2,3,64]{0,3,1,2:T(8,128)(2,1)}, u32[]{:S(2)}) copy-start(bf16[1024,2,3,64]{0,3,1,2:T(8,128)(2,1)} %copy-done.22) | copy-start | bytes 2359300 | tf_op jit(solution)/shard_map/while
  976.0 41.8 %reduce-scatter.22.cloned.1.call-start = ((), (), s32[]{:S(2)}) async-start(), calls=%async_computation.14 | async-start | bytes 491520
  976.8 51.5 %reduce-scatter.20.cloned.1.call-start = ((), (), s32[]{:S(2)}) async-start(), calls=%async_computation.13 | async-start | bytes 1228800
  999.3 11.0 copy-start.10
  1003.6 53.1 %reduce-scatter.16.cloned.1.call-start = ((), (), s32[]{:S(2)}) async-start(), calls=%async_computation.11 | async-start | bytes 1474560 | tf_op jit(solution)/shard_map/reduce_scatter | solution.py:316
  1010.3 75.2 %reduce-scatter.18.cloned.1.call-start = ((), (), s32[]{:S(2)}) async-start(), calls=%async_computation.12 | async-start | bytes 1474560 | tf_op jit(solution)/shard_map/reduce_scatter | solution.py:319
  1017.6 107.0 %all-reduce.14.cloned.1.call-start = ((), (), s32[]{:S(2)}) async-start(), calls=%async_computation.18 | async-start | bytes 1966080 | tf_op jit(solution)/shard_map/psum | solution.py:330
  1085.5 8.9 copy-start.25
  1085.5 8.9 copy-start.26
  1085.5 8.9 copy-start.30
  1085.5 265.0 %all-reduce.12.cloned.1.call-start = ((), (), s32[]{:S(2)}) async-start(), calls=%async_computation.17 | async-start | bytes 12582912 | tf_op jit(solution)/shard_map/psum | solution.py:296
  1098.6 308.4 %reduce-scatter.24.cloned.1.call-start = ((), (), s32[]{:S(2)}) async-start(), calls=%async_computation.15 | async-start | bytes 245760
  1350.6 8.7 copy-start.37
  1359.2 9.2 slice-start.2
  1373.0 8.2 copy-start.33
  1381.2 8.0 copy-start.39
  1381.2 8.0 copy-start.45
  1388.0 40.9 %reduce-scatter.26.cloned.1.call-start = ((), (), s32[]{:S(2)}) async-start(), calls=%async_computation.16 | async-start | bytes 245760
  1394.0 45.9 %copy-start.1 = (bf16[6,2,768]{2,1,0:T(2,128)(2,1)S(1)}, bf16[6,2,768]{2,1,0:T(2,128)(2,1)}, u32[]{:S(2)}) copy-start(bf16[6,2,768]{2,1,0:T(2,128)(2,1)} %param.20) | copy-start | bytes 55300
  (65 other events, 213.8 us)
Sparse Core Ops, SparseCore 0:
  10.4 21.5 all-gather.7
  201.1 17.7 all-gather.5
  699.1 26.1 all-gather.9
  806.4 26.0 reduce-scatter.27
  839.5 27.1 all-gather.9
  947.8 26.0 reduce-scatter.27
  979.9 20.8 reduce-scatter.21
  1003.8 24.4 reduce-scatter.19
  1031.0 25.6 reduce-scatter.15
  1059.8 25.6 reduce-scatter.17
  1388.1 18.6 reduce-scatter.23
  1409.1 19.7 reduce-scatter.25
Sparse Core Ops, SparseCore 1:
  198.8 222.9 all-reduce.7
  448.5 221.5 all-reduce.9
  1085.6 38.9 all-reduce.13
  1127.5 223.0 all-reduce.11
